TPU v7x, 512 devices: a whole 4x4x16 slice. The times are simulated.
512 devices in a mesh: samp: 64 (over z, y), hour: 8 (over x, core).
Axes of the slice: x: 4, y: 4, z: 16, core: 2. Of those that a mesh axis runs over, the one named last changes fastest.
Arguments:
- load_gap: float32 [3008, 4, 256], P('samp', None, 'hour'), may hold values from -21 to 21
- profiles: bfloat16 [4, 256, 131072], P(None, 'hour', 'samp'), may hold values from 0.019897461 to 0.3984375
- slot_of_sample: int32 [131072], P('samp'), may hold values from 0 to 1023, as said below
- slot_county: int32 [64, 1024], replicated, may hold values from 0 to 3007, as said below
Outputs:
- weight_step: float32 [4, 131072], P(None, ('samp', 'hour'))
- search_dir: float32 [4, 131072], P(None, ('samp', 'hour'))
- load_dir: float32 [3008, 4, 256], P('samp', None, 'hour')
Inputs may be any that keep to these rules, and one draw needn't show every extreme that they name: `slot_of_sample`: every slot 0 to 1023 of an index of samp is used by some sample of that index. `slot_county`: row d lists 1024 distinct counties in increasing order; county c is owned by index c // 47 of samp. At most 32 counties of a row have one owner; in every draw some owner has exactly 32 counties in every row.
All inputs are finite; a program needn't handle non-finite values.
Results may differ from a plain program's by a relative error of at most 0.00062.
Values sent between devices are 32-bit elements; how exact they have to be, the bound alone decides.
A program may use at most 64 MiB of HBM per device.

v0:
```python
import jax
import jax.numpy as jnp
from jax import lax
from jax.sharding import PartitionSpec as P

epsilon = 1e-06
PAD = 48


def two_pieces(x, axis):
    high = lax.reduce_precision(x, 8, 7)
    return jnp.concatenate([high, x - high], axis=axis).astype(jnp.bfloat16)


def local(load_gap, profiles, slot_of_sample, slot_county):
    owners = lax.axis_size("samp")
    hour_count = lax.axis_size("hour")
    owner_index = lax.axis_index("samp")
    hour_index = lax.axis_index("hour")
    use_count, hour_dev, samp_dev = profiles.shape
    per_owner = load_gap.shape[0]
    row_width = use_count * hour_dev
    share_len = samp_dev // hour_count
    space_count = float(per_owner * owners * row_width * hour_count)
    sample_count = float(use_count * samp_dev * owners)
    my_counties = lax.dynamic_index_in_dim(slot_county, owner_index, 0, keepdims=False)
    county = jnp.take(my_counties, slot_of_sample)
    place = county // per_owner * PAD + county % per_owner
    places = jnp.arange(owners * PAD, dtype=jnp.int32)
    onehot = (places[:, None] == place[None, :]).astype(jnp.bfloat16)
    wide = profiles.astype(jnp.float32)

    def padded(rows):
        return jnp.pad(rows, ((0, PAD - per_owner), (0, 0)))

    def backward(rows):
        everyone = lax.all_gather(padded(rows), "samp", tiled=True)
        square = jnp.sum(everyone * everyone)
        pieces = two_pieces(everyone, 1)
        spread = lax.dot_general(
            pieces, onehot, (((0,), (0,)), ((), ())), preferred_element_type=jnp.float32
        )
        spread = (spread[:row_width] + spread[row_width:]).reshape(use_count, hour_dev, samp_dev)
        partial = jnp.sum(wide * spread, axis=1)
        extra = jnp.zeros((1, samp_dev), jnp.float32).at[0, 0].set(square)
        total = lax.psum(jnp.concatenate([partial, extra], axis=0), "hour")
        return (total[:use_count], total[use_count, 0])

    def my_share(x):
        return lax.dynamic_slice_in_dim(x, hour_index * share_len, share_len, 1)

    gap_rows = load_gap.reshape(per_owner, row_width)
    plain, gap_total = backward(gap_rows)
    beta_one = jnp.sqrt(gap_total / space_count + epsilon)
    image = plain / beta_one
    weighted = (wide * image[:, None, :]).reshape(row_width, samp_dev)
    sums = lax.dot_general(
        onehot,
        two_pieces(weighted, 0),
        (((1,), (1,)), ((), ())),
        preferred_element_type=jnp.float32,
    )
    sums = (sums[:, :row_width] + sums[:, row_width:]).reshape(owners, PAD, row_width)
    mine = jnp.sum(image * image)
    row = jnp.arange(PAD, dtype=jnp.int32)[None, :, None]
    sums = jnp.where(row == per_owner, mine, sums).reshape(owners * PAD, row_width)
    owned = lax.psum_scatter(sums, "samp", scatter_dimension=0, tiled=True)
    alpha_one = jnp.sqrt(owned[per_owner, 0] / sample_count + epsilon)
    mismatch = owned[:per_owner] / alpha_one - alpha_one / beta_one * gap_rows
    back, mismatch_total = backward(mismatch)
    beta_two = jnp.sqrt(mismatch_total / space_count + epsilon)
    load_dir = mismatch / beta_two
    vector_one = image / alpha_one
    image_two = back / beta_two - beta_two * vector_one
    second_total = lax.psum(jnp.sum(image_two * image_two), "samp")
    alpha_two = jnp.sqrt(second_total / sample_count + epsilon)
    rho_value = jnp.sqrt(alpha_one * alpha_one + beta_two * beta_two)
    cosine = alpha_one / rho_value
    sine = beta_two / rho_value
    vector_share = my_share(vector_one)
    weight_step = cosine * beta_one / rho_value * vector_share
    search_dir = my_share(image_two) / alpha_two - sine * alpha_two / rho_value * vector_share
    return (weight_step, search_dir, load_dir.reshape(per_owner, use_count, hour_dev))


def solution(mesh):
    return jax.shard_map(
        local,
        mesh=mesh,
        in_specs=(P("samp", None, "hour"), P(None, "hour", "samp"), P("samp"), P()),
        out_specs=(P(None, ("samp", "hour")), P(None, ("samp", "hour")), P("samp", None, "hour")),
        check_vma=False,
    )
```

profile of v0, /device:TPU:8, one launch (start us, length us, event | category | flops | bytes accessed | tf_op | source)
XLA Modules:
  0.0 1211.6 jit_solution(9387377253845586838)
XLA Ops:
  7.2 0.9 copy.11
  8.2 0.6 pad.18
  8.9 0.1 broadcast_in_dim.29
  9.0 0.7 fusion.25
  9.7 8.6 gather_fusion
  18.3 0.6 compare_reduce_fusion
  19.0 136.3 %all-gather.3.cloned.1.call-done = f32[3072,128]{1,0:T(8,128)} async-done(((f32[48,128]{1,0:T(8,128)}), f32[3072,128]{1,0:T(8,128)}) %all-gather.3.cloned.1.call-update) | async-done | bytes 1572880 | tf_op jit(solution)/shard_map/all_gather | solution.py:37
  155.2 2.4 reduce-precision_convert_fusion.1
  159.0 4.9 fusion.2
  163.9 0.3 fusion.16
  164.2 24.1 %psum.21 = f32[5,2048]{1,0:T(8,128)S(1)} all-reduce(f32[5,2048]{1,0:T(8,128)S(1)} %select_maximum_fusion.1), channel_id=1, replica_groups=mesh['samp'=64,'hour'=8] {'hour'}, use_global_device_ids=true, to_apply=%region_3.4 | all-reduce | flops 10240 | bytes 81920 | tf_op jit(solution)/shard_map/psum | solution.py:46
  188.4 0.5 slice.85
  189.6 0.6 multiply_reduce_fusion.3
  190.2 0.1 convert_multiply_fusion.1
  190.3 0.1 reduce-precision_convert_fusion.2
  190.5 4.9 fusion.1
  195.4 3.1 fusion.8
  198.5 0.0 all-gather.5.cloned.1.call-start
  198.6 687.6 %reduce-scatter.2.cloned.1.call-done = f32[48,128]{1,0:T(8,128)} async-done(((f32[3072,128]{1,0:T(8,128)}), f32[48,128]{1,0:T(8,128)}) %reduce-scatter.2.cloned.1.call-update) | async-done | bytes 24592 | tf_op jit(solution)/shard_map/reduce_scatter | solution.py:67
  886.2 1.2 slice.88
  888.1 0.7 fusion.21
  888.9 0.6 pad.19
  889.5 138.2 %all-gather.5.cloned.1.call-done = f32[3072,128]{1,0:T(8,128)} async-done(((f32[48,128]{1,0:T(8,128)}), f32[3072,128]{1,0:T(8,128)}) %all-gather.5.cloned.1.call-update) | async-done | bytes 1572880 | tf_op jit(solution)/shard_map/all_gather | solution.py:37
  1027.7 2.4 reduce-precision_convert_fusion
  1031.4 4.9 fusion
  1036.4 0.3 fusion.17
  1036.7 23.9 %psum.22 = f32[5,2048]{1,0:T(8,128)S(1)} all-reduce(f32[5,2048]{1,0:T(8,128)S(1)} %select_maximum_fusion), channel_id=1, replica_groups=mesh['samp'=64,'hour'=8] {'hour'}, use_global_device_ids=true, to_apply=%region_8.9 | all-reduce | flops 10240 | bytes 81920 | tf_op jit(solution)/shard_map/psum | solution.py:46
  1060.6 0.5 slice.92
  1062.0 0.6 multiply_reduce_fusion.2
  1062.6 140.4 %psum.23 = f32[]{:T(128)} all-reduce(f32[]{:T(128)} %get-tuple-element.33), channel_id=1, replica_groups=mesh['samp'=64,'hour'=8] {'samp'}, use_global_device_ids=true, to_apply=%region_10.11 | all-reduce | flops 1 | bytes 8 | tf_op jit(solution)/shard_map/psum | solution.py:75
  1203.7 0.7 copy.12
  1204.5 0.6 divide_subtract_fusion.1
  (18 shorter events, 0.2 us)
Async XLA Ops:
  7.2 1.8 copy-start
  7.2 148.1 %all-gather.3.cloned.1.call-start = ((), (), s32[]{:S(2)}) async-start(), calls=%async_computation.1 | async-start | bytes 1597440 | tf_op jit(solution)/shard_map/all_gather | solution.py:37
  8.8 877.4 %reduce-scatter.2.cloned.1.call-start = ((), (), s32[]{:S(2)}) async-start(), calls=%async_computation.2 | async-start | bytes 1597440 | tf_op jit(solution)/shard_map/reduce_scatter | solution.py:67
  9.7 9.2 copy-start.2
  159.0 5.0 copy-start.1
  198.5 829.1 %all-gather.5.cloned.1.call-start = ((), (), s32[]{:S(2)}) async-start(), calls=%async_computation.3 | async-start | bytes 1597440 | tf_op jit(solution)/shard_map/all_gather | solution.py:37
Sparse Core Ops, SparseCore 0:
  11.5 143.6 all-gather.2
  198.7 687.4 reduce-scatter.1
  890.1 137.4 all-gather.4
where the time goes:
time: 1210 us
  waiting for transfers between devices  962 us (80%)
  blocking collectives  188 us (16%)
  between operations  19.5 us (2%)
  matrix products  14.8 us (1%)
  local copies, waits for them, and re-layouts  13.8 us (1%)
  other arithmetic  12.8 us (1%)
    reduce_scatter x1, waiting for transfers between devices, local(): owned = lax.psum_scatter(sums, 'samp', scatter_dimension=0, tiled=True)  688 us
    all_gather x2, waiting for transfers between devices, backward(): everyone = lax.all_gather(padded(rows), 'samp', tiled=True)  274 us
    psum x1, blocking collectives, local(): second_total = lax.psum(jnp.sum(image_two * image_two), 'samp')  140 us
    psum x2, blocking collectives, backward(): total = lax.psum(jnp.concatenate([partial, extra], axis=0), 'hour')  48.1 us
  transfers between devices with their start and end apart: 3, of which 3 were waited for; matrix products, arithmetic and copies ran while one was open for 1% of the time, Pallas kernels for 0%

commit v1 on v0

--- a/solution.py
+++ b/solution.py
@@ -5,6 +5,15 @@
 
 epsilon = 1e-06
 PAD = 48
+
+
+def obtain_threads(frame_in, named_axis):
+    return jnp.concatenate(
+        lax.all_to_all(
+            jnp.stack([frame_in for _ in range(lax.axis_size(named_axis))]), named_axis, 0, 0
+        ),
+        axis=0,
+    )
 
 
 def two_pieces(x, axis):
@@ -34,7 +43,7 @@
         return jnp.pad(rows, ((0, PAD - per_owner), (0, 0)))
 
     def backward(rows):
-        everyone = lax.all_gather(padded(rows), "samp", tiled=True)
+        everyone = obtain_threads(padded(rows), named_axis="samp")
         square = jnp.sum(everyone * everyone)
         pieces = two_pieces(everyone, 1)
         spread = lax.dot_general(

time: 1210 us -> 1100 us (0.909)
  waiting for transfers between devices: 962 us -> 817 us
  starting transfers between devices: 0.12 us -> 31.3 us
    all_gather x2 -> x0, waiting for transfers between devices: 274 us -> none  [backward(): everyone = lax.all_gather(padded(rows), 'samp', tiled=True)]
    all_to_all x0 -> x2, waiting for transfers between devices: none -> 134 us  [obtain_threads(): lax.all_to_all(jnp.stack([frame_in for _ in range(lax.axis_size(named_axi...]
    all_to_all x0 -> x2, starting transfers between devices: none -> 31.3 us  [obtain_threads(): lax.all_to_all(jnp.stack([frame_in for _ in range(lax.axis_size(named_axi...]
where the time goes in v1:
time: 1100 us
  waiting for transfers between devices  817 us (74%)
  blocking collectives  187 us (17%)
  starting transfers between devices  31.3 us (3%)
  between operations  19.9 us (2%)
  local copies, waits for them, and re-layouts  15.1 us (1%)
  matrix products  14.8 us (1%)
    reduce_scatter x1, waiting for transfers between devices, local(): owned = lax.psum_scatter(sums, 'samp', scatter_dimension=0, tiled=True)  683 us
    psum x1, blocking collectives, local(): second_total = lax.psum(jnp.sum(image_two * image_two), 'samp')  139 us
    all_to_all x2, waiting for transfers between devices, obtain_threads(): lax.all_to_all(jnp.stack([frame_in for _ in range(lax.axis_size(named_axi...  134 us
    psum x2, blocking collectives, backward(): total = lax.psum(jnp.concatenate([partial, extra], axis=0), 'hour')  48.1 us
    all_to_all x2, starting transfers between devices, obtain_threads(): lax.all_to_all(jnp.stack([frame_in for _ in range(lax.axis_size(named_axi...  31.3 us
  transfers between devices with their start and end apart: 3, of which 3 were waited for; matrix products, arithmetic and copies ran while one was open for 1% of the time, Pallas kernels for 0%

profile of v1, /device:TPU:8, one launch (start us, length us, event | category | flops | bytes accessed | tf_op | source)
XLA Modules:
  0.0 1095.7 jit_solution(9769979153117005803)
XLA Ops:
  7.2 1.0 copy.13
  8.2 1.3 stack.4
  9.4 18.7 %all-to-all-start = ((f32[64,48,128]{2,1,0:T(8,128)}), f32[64,48,128]{2,1,0:T(8,128)S(1)}, u32[]{:S(2)}, u32[]{:S(2)}) async-start(f32[64,48,128]{2,1,0:T(8,128)} %stack.4), calls=%async_computation | async-start | bytes 3145728 | tf_op jit(solution)/shard_map/all_to_all | solution.py:12
  28.4 8.6 gather_fusion
  37.0 0.6 compare_reduce_fusion
  37.6 68.2 %all-to-all-done = f32[64,48,128]{2,1,0:T(8,128)S(1)} async-done(((f32[64,48,128]{2,1,0:T(8,128)}), f32[64,48,128]{2,1,0:T(8,128)S(1)}, u32[]{:S(2)}, u32[]{:S(2)}) %all-to-all-start) | async-done | bytes 1572896 | tf_op jit(solution)/shard_map/all_to_all | solution.py:12
  105.8 1.0 multiply_reduce_fusion.1
  108.1 0.2 reduce-precision_convert_fusion.1
  108.4 4.9 fusion.2
  113.3 0.3 fusion.16
  113.6 24.1 %psum.21 = f32[5,2048]{1,0:T(8,128)S(1)} all-reduce(f32[5,2048]{1,0:T(8,128)S(1)} %select_maximum_fusion.1), channel_id=1, replica_groups=mesh['samp'=64,'hour'=8] {'hour'}, use_global_device_ids=true, to_apply=%region_3.4 | all-reduce | flops 10240 | bytes 81920 | tf_op jit(solution)/shard_map/psum | solution.py:55
  137.7 0.5 slice.85
  139.0 0.6 multiply_reduce_fusion.3
  139.7 0.1 reduce-precision_convert_fusion.2
  139.8 4.9 fusion.1
  144.8 3.1 fusion.8
  147.9 683.4 %reduce-scatter.2.cloned.1.call-done = f32[48,128]{1,0:T(8,128)} async-done(((f32[3072,128]{1,0:T(8,128)}), f32[48,128]{1,0:T(8,128)}) %reduce-scatter.2.cloned.1.call-update) | async-done | bytes 24592 | tf_op jit(solution)/shard_map/reduce_scatter | solution.py:76
  831.3 1.2 slice.88
  833.3 0.7 fusion.21
  834.0 1.3 stack.5
  835.3 12.5 %all-to-all-start.1 = ((f32[64,48,128]{2,1,0:T(8,128)}), f32[64,48,128]{2,1,0:T(8,128)S(1)}, u32[]{:S(2)}, u32[]{:S(2)}) async-start(f32[64,48,128]{2,1,0:T(8,128)} %stack.5), calls=%async_computation.2 | async-start | bytes 3145728 | tf_op jit(solution)/shard_map/all_to_all | solution.py:12
  847.8 65.9 %all-to-all-done.1 = f32[64,48,128]{2,1,0:T(8,128)S(1)} async-done(((f32[64,48,128]{2,1,0:T(8,128)}), f32[64,48,128]{2,1,0:T(8,128)S(1)}, u32[]{:S(2)}, u32[]{:S(2)}) %all-to-all-start.1) | async-done | bytes 1572896 | tf_op jit(solution)/shard_map/all_to_all | solution.py:12
  913.7 1.1 multiply_reduce_fusion
  916.1 0.2 reduce-precision_convert_fusion
  916.4 4.9 fusion
  921.3 0.3 fusion.17
  921.6 23.9 %psum.22 = f32[5,2048]{1,0:T(8,128)S(1)} all-reduce(f32[5,2048]{1,0:T(8,128)S(1)} %select_maximum_fusion), channel_id=1, replica_groups=mesh['samp'=64,'hour'=8] {'hour'}, use_global_device_ids=true, to_apply=%region_8.9 | all-reduce | flops 10240 | bytes 81920 | tf_op jit(solution)/shard_map/psum | solution.py:55
  945.6 0.5 slice.92
  947.0 0.6 multiply_reduce_fusion.2
  947.6 139.1 %psum.23 = f32[]{:T(128)} all-reduce(f32[]{:T(128)} %get-tuple-element.36), channel_id=1, replica_groups=mesh['samp'=64,'hour'=8] {'samp'}, use_global_device_ids=true, to_apply=%region_10.11 | all-reduce | flops 1 | bytes 8 | tf_op jit(solution)/shard_map/psum | solution.py:84
  1087.5 0.7 copy.14
  1088.2 0.6 divide_subtract_fusion.1
  (20 shorter events, 0.4 us)
Async XLA Ops:
  7.2 21.2 %copy-start = (s32[64,1024]{1,0:T(8,128)S(1)}, s32[64,1024]{1,0:T(8,128)}, u32[]{:S(2)}) copy-start(s32[64,1024]{1,0:T(8,128)} %param.11) | copy-start | bytes 786436
  8.2 20.2 %copy-start.2 = (s32[2048]{0:T(1024)S(1)}, s32[2048]{0:T(1024)}, u32[]{:S(2)}) copy-start(s32[2048]{0:T(1024)} %param.10) | copy-start | bytes 24580
  9.4 96.4 %all-to-all-start = ((f32[64,48,128]{2,1,0:T(8,128)}), f32[64,48,128]{2,1,0:T(8,128)S(1)}, u32[]{:S(2)}, u32[]{:S(2)}) async-start(f32[64,48,128]{2,1,0:T(8,128)} %stack.4), calls=%async_computation | async-start | bytes 3145728 | tf_op jit(solution)/shard_map/all_to_all | solution.py:12
  28.2 803.2 %reduce-scatter.2.cloned.1.call-start = ((), (), s32[]{:S(2)}) async-start(), calls=%async_computation.3 | async-start | bytes 1597440 | tf_op jit(solution)/shard_map/reduce_scatter | solution.py:76
  108.4 5.0 copy-start.1
  835.3 78.4 %all-to-all-start.1 = ((f32[64,48,128]{2,1,0:T(8,128)}), f32[64,48,128]{2,1,0:T(8,128)S(1)}, u32[]{:S(2)}, u32[]{:S(2)}) async-start(f32[64,48,128]{2,1,0:T(8,128)} %stack.5), calls=%async_computation.2 | async-start | bytes 3145728 | tf_op jit(solution)/shard_map/all_to_all | solution.py:12
Sparse Core Ops, SparseCore 0:
  148.0 683.2 reduce-scatter.1
